TPU v7x, 128 devices: a whole 4x4x4 slice. The times are simulated.
128 devices in a mesh: dp: 8 (over z, y_lo), shard: 16 (over x, y_hi, core).
Axes of the slice: x: 4, y: 4 (y_hi: 2, y_lo: 2; y = y_hi * 2 + y_lo), z: 4, core: 2. Of those that a mesh axis runs over, the one named last changes fastest.
Arguments:
- prefill_x: bfloat16 [98304, 1536], P(('dp', 'shard')), may hold values from -6 to 6
- decode_x: bfloat16 [64, 1536], P('dp'), may hold values from -6 to 6
- norm_gain: bfloat16 [1536], P(('dp', 'shard')), may hold values from 0.099609375 to 1.8984375
- wqkv: bfloat16 [1536, 3072], P(('dp', 'shard')), may hold values from -0.15625 to 0.15625
- wo: bfloat16 [1536, 1536], P(('dp', 'shard')), may hold values from -0.15625 to 0.15625
- k_cache: bfloat16 [64, 8192, 768], P('dp', 'shard'), may hold values from -360 to 360
- v_cache: bfloat16 [64, 8192, 768], P('dp', 'shard'), may hold values from -6 to 6
- cache_len: int32 [64], P('dp'), may hold values from 1 to 8192, as said below
Outputs:
- prefill_out: bfloat16 [98304, 1536], P(('dp', 'shard'))
- decode_out: bfloat16 [64, 1536], P('dp')
Inputs may be any that keep to these rules, and one draw needn't show every extreme that they name: `cache_len`: some request has exactly 8192 cached positions.
All inputs are finite; a program needn't handle non-finite values.
Results may differ from a plain program's by a relative error of at most 0.0095.
The roundings to bfloat16 on the way count: a program that leaves them out, or rounds other values in their place, can miss the bound.
Values may be sent and summed in bfloat16 or wider, within the bound.
A program may use at most 128 MiB of HBM per device.

v0:
```python
import jax
import jax.numpy as jnp
from jax import lax
from jax.sharding import PartitionSpec as P

H = 16
KV = 8
HD = 96


THETA = 100000.0
EPS = 1e-05
NEGATIVE = -1e30


def rotate(tensor, positions):
    half_width = tensor.shape[-1] // 2
    frequency = jnp.power(
        THETA, -jnp.arange(half_width, dtype=jnp.float32) * (2.0 / tensor.shape[-1])
    )
    angles = positions.astype(jnp.float32)[:, None] * frequency[None, :]
    cosine = jnp.cos(angles)[:, None, :]
    sine_part = jnp.sin(angles)[:, None, :]
    leading = tensor[..., :half_width]
    trailing = tensor[..., half_width:]
    return jnp.concatenate(
        [leading * cosine - trailing * sine_part, trailing * cosine + leading * sine_part], axis=-1
    )


def causal_stretch(queries, new_keys, new_values):
    row_count = queries.shape[0]
    group_size = H // KV
    query_heads = jnp.moveaxis(queries.reshape(row_count, KV, group_size, HD), 1, 0)
    key_heads = jnp.moveaxis(new_keys, 1, 0)
    value_heads = jnp.moveaxis(new_values, 1, 0)
    indices = jnp.arange(row_count, dtype=jnp.int32)
    allowed = indices[None, :] <= indices[:, None]

    def one_head(operands):
        query_head, key_head, value_head = operands
        scores = jnp.einsum(
            "qgd,sd->gqs", query_head, key_head, preferred_element_type=jnp.float32
        ) * HD ** (-0.5)
        scores = jnp.where(allowed[None], scores, NEGATIVE)
        highest = jnp.max(scores, axis=-1, keepdims=True)
        expanded = jnp.exp(scores - highest)
        weights = (expanded / jnp.sum(expanded, axis=-1, keepdims=True)).astype(jnp.bfloat16)
        return jnp.einsum(
            "gqs,sd->qgd", weights, value_head, preferred_element_type=jnp.float32
        ).astype(jnp.bfloat16)

    attended = lax.map(one_head, (query_heads, key_heads, value_heads))
    return jnp.moveaxis(attended, 0, 1).reshape(row_count, H * HD)


def per_device(prefill_x, decode_x, norm_gain, wqkv, wo, k_cache, v_cache, cache_len):
    stretch_rows = prefill_x.shape[0]
    request_count = decode_x.shape[0]
    stacked = jnp.concatenate([prefill_x, decode_x], axis=0).astype(jnp.float32)
    scaled = stacked * lax.rsqrt(jnp.mean(stacked * stacked, axis=-1, keepdims=True) + EPS)
    weight_rows = lax.all_gather(wqkv, ("dp", "shard"), axis=0, tiled=True)
    gain_rows = lax.all_gather(norm_gain, ("dp", "shard"), axis=0, tiled=True)
    columns = scaled
    left_side = (columns * gain_rows.astype(jnp.float32)[None, :]).astype(jnp.bfloat16)
    united_rows = jnp.dot(left_side, weight_rows, preferred_element_type=jnp.float32)
    row_total = united_rows.shape[0]
    positions = jnp.concatenate([jnp.arange(stretch_rows, dtype=jnp.int32), cache_len])
    queries = rotate(united_rows[:, : H * HD].reshape(row_total, H, HD), positions).astype(
        jnp.bfloat16
    )
    new_keys = rotate(
        united_rows[:, H * HD : (H + KV) * HD].reshape(row_total, KV, HD), positions
    ).astype(jnp.bfloat16)
    new_values = united_rows[:, (H + KV) * HD :].reshape(row_total, KV, HD).astype(jnp.bfloat16)
    prefill_mix = causal_stretch(
        queries[:stretch_rows], new_keys[:stretch_rows], new_values[:stretch_rows]
    )
    score_scale = HD ** (-0.5)
    cache_span = k_cache.shape[1]
    decode_queries = queries[stretch_rows:].reshape(request_count, KV, H // KV, HD)
    self_keys = new_keys[stretch_rows:]
    self_values = new_values[stretch_rows:]
    key_blocks = k_cache.reshape(request_count, cache_span, KV, HD)
    value_blocks = v_cache.reshape(request_count, cache_span, KV, HD)
    scores = (
        jnp.einsum(
            "rkgd,rpkd->rkgp", decode_queries, key_blocks, preferred_element_type=jnp.float32
        )
        * score_scale
    )
    positions_here = lax.axis_index("shard") * cache_span + jnp.arange(cache_span, dtype=jnp.int32)
    live_mask = positions_here[None, None, None, :] < cache_len[:, None, None, None]
    scores = jnp.where(live_mask, scores, NEGATIVE)
    block_peaks = jnp.max(scores, axis=-1)
    expanded = jnp.where(live_mask, jnp.exp(scores - block_peaks[..., None]), 0.0)
    partial_totals = jnp.sum(expanded, axis=-1)
    partial_sums = jnp.einsum(
        "rkgp,rpkd->rkgd",
        expanded.astype(jnp.bfloat16),
        value_blocks,
        preferred_element_type=jnp.float32,
    )
    group_top = lax.pmax(block_peaks, "shard")
    rescale = jnp.exp(block_peaks - group_top)
    numer_all, denom_all = lax.psum(
        (partial_sums * rescale[..., None], partial_totals * rescale), "shard"
    )
    self_scores = (
        jnp.einsum("rkgd,rkd->rkg", decode_queries, self_keys, preferred_element_type=jnp.float32)
        * score_scale
    )
    overall = jnp.maximum(group_top, self_scores)
    old_weight = jnp.exp(group_top - overall)
    own_weight = jnp.exp(self_scores - overall)
    numerator = (
        numer_all * old_weight[..., None]
        + own_weight[..., None] * self_values.astype(jnp.float32)[:, :, None, :]
    )
    denominator = denom_all * old_weight + own_weight
    decode_mix = (
        (numerator / denominator[..., None]).reshape(request_count, H * HD).astype(jnp.bfloat16)
    )
    attended = jnp.concatenate([prefill_mix, decode_mix], axis=0)
    columns = attended
    projected = jnp.dot(
        columns,
        lax.all_gather(wo, ("dp", "shard"), axis=0, tiled=True),
        preferred_element_type=jnp.float32,
    )
    return (
        projected[:stretch_rows].astype(jnp.bfloat16),
        projected[stretch_rows:].astype(jnp.bfloat16),
    )


def solution(mesh):
    in_specs = (
        P(("dp", "shard"), None),
        P("dp", None),
        P(("dp", "shard")),
        P(("dp", "shard"), None),
        P(("dp", "shard"), None),
        P("dp", "shard", None),
        P("dp", "shard", None),
        P("dp"),
    )
    out_specs = (P(("dp", "shard"), None), P("dp", None))
    return jax.shard_map(
        per_device, mesh=mesh, in_specs=in_specs, out_specs=out_specs, check_vma=False
    )
```

profile of v0, /device:TPU:0, one launch (start us, length us, event | category | flops | bytes accessed | tf_op | source)
XLA Modules:
  0.0 696.2 jit_solution(7698980589550562163)
XLA Ops:
  7.2 0.7 all-gather.7.cloned.1.call-update
  7.9 0.7 all-gather.5.cloned.1.call-update
  8.7 0.9 dynamic-update-slice
  9.5 68.3 %all-reduce = bf16[1536]{0:T(1024)(128)(2,1)S(1)} all-reduce(bf16[1536]{0:T(1024)(128)(2,1)S(1)} %dynamic-update-slice), channel_id=1, replica_groups=mesh['dp'=8,'shard'=16] {'dp','shard'}, use_global_device_ids=true, to_apply=%add | all-reduce | flops 1536 | bytes 6144
  77.8 8.6 %copy.33 = bf16[8,512,768]{1,2,0:T(8,128)(2,1)} copy(bf16[8,512,768]{2,1,0:T(8,128)(2,1)} %param.15) | data formatting | bytes 12582912 | tf_op args[5]
  86.5 8.8 %copy.34 = bf16[8,512,768]{1,2,0:T(8,128)(2,1)} copy(bf16[8,512,768]{2,1,0:T(8,128)(2,1)} %param.16) | data formatting | bytes 12582912 | tf_op args[6]
  95.4 0.5 fusion.41
  96.0 0.7 multiply_cosine_fusion
  96.7 115.6 %all-gather.7.cloned.1.call-done = bf16[128,12,1536]{2,1,0:T(8,128)(2,1)} async-done(((bf16[1,12,1536]{2,1,0:T(8,128)(2,1)}), bf16[128,12,1536]{2,1,0:T(8,128)(2,1)}) %all-gather.7.cloned.1.call-update) | async-done | bytes 4718608 | tf_op jit(solution)/shard_map/all_gather | solution.py:128
  212.3 8.2 %reshape.162 = bf16[1536,1536]{1,0:T(8,128)(2,1)} reshape(bf16[128,12,1536]{2,1,0:T(8,128)(2,1)} %all-gather.7.cloned.1.call-done) | data formatting | bytes 9437184
  220.4 199.3 %all-gather.5.cloned.1.call-done = bf16[128,12,3072]{2,1,0:T(8,128)(2,1)} async-done(((bf16[1,12,3072]{2,1,0:T(8,128)(2,1)}), bf16[128,12,3072]{2,1,0:T(8,128)(2,1)}) %all-gather.5.cloned.1.call-update) | async-done | bytes 9437200 | tf_op jit(solution)/shard_map/all_gather | solution.py:62
  419.7 13.7 %reshape.160 = bf16[1536,3072]{1,0:T(8,128)(2,1)} reshape(bf16[128,12,3072]{2,1,0:T(8,128)(2,1)} %all-gather.5.cloned.1.call-done) | data formatting | bytes 18874368
  433.4 12.3 %fusion.77 = (bf16[776,3072]{1,0:T(8,128)(2,1)}, f32[776,3072]{1,0:T(8,128)S(1)}) fusion(bf16[1536,3072]{1,0:T(8,128)(2,1)} %reshape.160, f32[1536]{0:T(1024)S(1)} %convert_element_type.48, f32[776]{0:T(1024)S(1)} %add_rsqrt_fusion, bf16[8,1536]{1,0:T(8,128)(2,1)S(1)} %copy-done.1, bf16[768,1536]{1,0:T(8,128)(2,1)S(1)} %copy-done), kind=kOutput, calls=%fused_computation.86 | convolution fusion | flops 7333982208 | bytes 26133536 | tf_op jit(solution)/shard_map/dot_general | solution.py:66
  445.7 2.7 slice.73
  448.5 1.6 slice.68
  450.1 5.9 copy.31
  456.0 3.4 subtract_convert_fusion
  459.4 1.7 fusion.51
  461.1 2.2 copy.30
  463.2 0.4 subtract_convert_fusion.1
  463.8 0.7 slice_convert_fusion
  464.5 1.3 slice.67
  466.0 3.8 fusion.76
  469.8 67.2 %pmax.7 = f32[8,8,2]{2,1,0:T(8,128)S(1)} all-reduce(f32[8,8,2]{2,1,0:T(8,128)S(1)} %get-tuple-element.72), channel_id=1, replica_groups=mesh['dp'=8,'shard'=16] {'shard'}, use_global_device_ids=true, to_apply=%region_6.7 | all-reduce | flops 128 | bytes 1024 | tf_op jit(solution)/shard_map/pmax | solution.py:104
  536.9 0.4 fusion.58
  537.8 4.6 convolution_multiply_fusion.1
  542.4 65.7 %all-reduce.1 = (f32[8,8,2,96]{3,2,1,0:T(2,128)S(1)}, f32[8,8,2]{2,1,0:T(8,128)S(1)}) all-reduce(f32[8,8,2,96]{3,2,1,0:T(2,128)S(1)} %convolution_multiply_fusion.1, f32[8,8,2]{2,1,0:T(8,128)S(1)} %get-tuple-element.62), channel_id=1, replica_groups=mesh['dp'=8,'shard'=16] {'shard'}, use_global_device_ids=true, to_apply=%region_7.8 | all-reduce | flops 12416 | bytes 99328 | tf_op jit(solution)/shard_map/psum | solution.py:106
  608.6 1.5 copy.29
  610.1 70.1 %while.11 = (s32[]{:T(128)}, bf16[8,768,2,96]{1,3,2,0:T(8,128)(2,1)}, bf16[8,768,96]{1,2,0:T(8,128)(2,1)}, bf16[8,768,96]{1,2,0:T(8,128)(2,1)S(1)}, bf16[8,768,2,96]{1,3,2,0:T(8,128)(2,1)}, /*index=5*/s32[]{:T(128)}) while((s32[]{:T(128)}, bf16[8,768,2,96]{1,3,2,0:T(8,128)(2,1)}, bf16[8,768,96]{1,2,0:T(8,128)(2,1)}, ...), condition=%wide.region_4.5_spmd.clone, body=%wide.region_1.4_spmd.clone.sunk | while | flops 460800768 | bytes 11515973 | solution.py:53
  610.3 4.9 fusion.94
  615.2 3.7 fusion.95
  619.0 4.9 fusion.94
  624.0 3.7 fusion.95
  627.8 4.9 fusion.94
  632.7 3.7 fusion.95
  636.6 4.9 fusion.94
  641.5 3.7 fusion.95
  645.3 4.9 fusion.94
  650.3 3.7 fusion.95
  654.1 4.9 fusion.94
  659.0 3.7 fusion.95
  662.9 4.9 fusion.94
  667.8 3.7 fusion.95
  671.6 4.9 fusion.94
  676.6 3.7 fusion.95
  680.2 7.0 %convolution_convert_fusion = bf16[776,1536]{1,0:T(8,128)(2,1)S(1)} fusion(bf16[1536,1536]{1,0:T(8,128)(2,1)} %reshape.162, bf16[8,1536]{0,1:T(8,128)(2,1)S(1)} %bitcast.92, bf16[768,1536]{0,1:T(8,128)(2,1)} %bitcast.98), kind=kOutput, calls=%fused_computation.36 | convolution fusion | flops 3667587072 | bytes 9486336 | tf_op jit(solution)/shard_map/dot_general | solution.py:126
  687.2 1.6 slice.79
  688.8 0.6 slice.80
  (36 shorter events, 3.0 us)
Async XLA Ops:
  7.2 205.1 %all-gather.7.cloned.1.call-start = ((), (), s32[]{:S(2)}) async-start(), calls=%async_computation.1 | async-start | bytes 6340608 | tf_op jit(solution)/shard_map/all_gather | solution.py:128
  7.9 411.8 %all-gather.5.cloned.1.call-start = ((), (), s32[]{:S(2)}) async-start(), calls=%async_computation | async-start | bytes 12681216 | tf_op jit(solution)/shard_map/all_gather | solution.py:62
  86.5 8.9 %copy-start.2 = (s32[8]{0:T(128)S(1)}, s32[8]{0:T(128)}, u32[]{:S(2)}) copy-start(s32[8]{0:T(128)} %param.17) | copy-start | bytes 100
  86.5 8.9 %copy-start = (bf16[768,1536]{1,0:T(8,128)(2,1)S(1)}, bf16[768,1536]{1,0:T(8,128)(2,1)}, u32[]{:S(2)}) copy-start(bf16[768,1536]{1,0:T(8,128)(2,1)} %param.10) | copy-start | bytes 7077892
  86.5 8.9 %copy-start.1 = (bf16[8,1536]{1,0:T(8,128)(2,1)S(1)}, bf16[8,1536]{1,0:T(8,128)(2,1)}, u32[]{:S(2)}) copy-start(bf16[8,1536]{1,0:T(8,128)(2,1)} %param.11) | copy-start | bytes 73732
Sparse Core Ops, SparseCore 0:
  9.7 202.5 all-gather.6
  214.0 205.6 all-gather.4
where the time goes:
time: 698 us; the launch traced here: 696 us
  waiting for transfers between devices  316 us (45%)
  blocking collectives  201 us (29%)
  matrix products  96.6 us (14%)
  local copies, waits for them, and re-layouts  58.2 us (8%)
  between operations  14.2 us (2%)
  other arithmetic  9.72 us (1%)
    all_gather x1, waiting for transfers between devices, per_device(): weight_rows = lax.all_gather(wqkv, ('dp', 'shard'), axis=0, tiled=True)  199 us
    all_gather x1, waiting for transfers between devices, per_device(): lax.all_gather(wo, ('dp', 'shard'), axis=0, tiled=True)  116 us
    unnamed x1, blocking collectives  68.3 us
    pmax x1, blocking collectives, per_device(): group_top = lax.pmax(block_peaks, 'shard')  67.2 us
    psum x1, blocking collectives, per_device(): lax.psum((partial_sums * rescale[..., None], partial_totals * rescale), '...  65.7 us
    unnamed x12, local copies, waits for them, and re-layouts  40.2 us
    sub x8, matrix products, one_head(): expanded = jnp.exp(scores - highest)  39.4 us
    dot_general x8, matrix products, one_head(): jnp.einsum('gqs,sd->qgd', weights, value_head, preferred_element_type=jnp...  29.3 us
  transfers between devices with their start and end apart: 2, of which 2 were waited for; matrix products, arithmetic and copies ran while one was open for 4% of the time, Pallas kernels for 0%

commit v1 on v0

v1 whole, which is shorter than its diff:
```python
import jax
import jax.numpy as jnp
from jax import lax
from jax.experimental import pallas as pl
from jax.experimental.pallas import tpu as pltpu
from jax.sharding import PartitionSpec as P

MESH = pl.DeviceIdType.MESH
H, KV, HD = 16, 8, 96
THETA, EPS, NEGATIVE = 100000.0, 1e-05, -1e30
SCALE = HD ** (-0.5)
ORDERS = (("x", "y", "z"), ("y", "z", "x"), ("z", "x", "y"))
N_CHUNK = 3
BF, F32 = jnp.bfloat16, jnp.float32


def coords():
    dp = lax.axis_index("dp"); sh = lax.axis_index("shard")
    core = sh % 2; yhi = (sh // 2) % 2; x = sh // 4
    ylo = dp % 2; z = dp // 2
    return {"x": x, "y": yhi * 2 + ylo, "z": z}, core

def device(c, core):
    return (c["z"] * 2 + c["y"] % 2, c["x"] * 4 + (c["y"] // 2) * 2 + core)

def moved(c, axis, by):
    d = dict(c); d[axis] = (c[axis] + by + 4) % 4
    return d

def block(ref, c, free):
    full = slice(None)
    z = full if "z" in free else c["z"]
    x = full if "x" in free else c["x"]
    ylo = full if "y" in free else c["y"] % 2
    yhi = full if "y" in free else c["y"] // 2
    return ref.at[z, ylo, x, yhi]

class Gather:
    def __init__(self, w, ssem, rsem, dsem_s, dsem_r):
        self.w, self.ssem, self.rsem, self.ds, self.dr = w, ssem, rsem, dsem_s, dsem_r
        self.c, self.core = coords()
        self.sent = []

    def part(self, t, k, core=None):
        core = self.core if core is None else core
        return self.w.at[t * 6 + core * 3 + k]

    def copy(self, t, k, f, s, right, origin):
        order = ORDERS[k]; axis = order[f]
        b = block(self.part(t, k), origin, order[:f])
        if s == 1:
            b = b.at[..., pl.ds(0 if right else 128, 128)]
        i = (((t * 3 + k) * 3 + f) * 2 + s) * 2 + (0 if right else 1)
        return pltpu.make_async_remote_copy(
            src_ref=b, dst_ref=b, send_sem=self.ssem.at[i], recv_sem=self.rsem.at[i],
            device_id=device(moved(self.c, axis, 1 if right else -1), self.core), device_id_type=MESH)

    def send(self, t, f, s):
        for k in range(3):
            axis = ORDERS[k][f]
            for right in (True, False):
                origin = self.c if s == 0 else moved(self.c, axis, -1 if right else 1)
                cp = self.copy(t, k, f, s, right, origin)
                cp.start(); self.sent.append(cp)

    def recv(self, t, f, s):
        for k in range(3):
            axis = ORDERS[k][f]
            for right in (True, False):
                by = (1 + s) * (-1 if right else 1)
                self.copy(t, k, f, s, right, moved(self.c, axis, by)).wait_recv()

    def d2d(self, t, k, j, core):
        order = ORDERS[k]
        b = block(self.part(t, k, core), moved(self.c, order[2], (0, -1, 1, 2)[j]), order[:2])
        i = (t * 3 + k) * 4 + j
        return pltpu.make_async_remote_copy(
            src_ref=b, dst_ref=b, send_sem=self.ds.at[i], recv_sem=self.dr.at[i],
            device_id=device(self.c, 1 - self.core), device_id_type=MESH)

    def give(self, t, js):
        for k in range(3):
            for j in js:
                cp = self.d2d(t, k, j, self.core); cp.start(); self.sent.append(cp)

    def take(self, t):
        for k in range(3):
            for j in range(4):
                self.d2d(t, k, j, 1 - self.core).wait_recv()

    def step(self, t, n):
        if n > 0:
            self.recv(t, (n - 1) // 2, (n - 1) % 2)
        if n < 6:
            self.send(t, n // 2, n % 2)
        if n == 4:
            self.give(t, (0,))
        if n == 5:
            self.give(t, (1, 2))
        if n == 6:
            self.give(t, (3,))

    def finish(self):
        for cp in self.sent:
            cp.wait_send()

def neighbours(c, core):
    out = [device(c, 1 - core)]
    for axis in ("x", "y", "z"):
        for by in (1, -1):
            out.append(device(moved(c, axis, by), core))
    return out + [partner(c, core, 1), partner(c, core, 3)]

def barrier(c, core):
    sem = pltpu.get_barrier_semaphore()
    for d in neighbours(c, core):
        pl.semaphore_signal(sem, inc=1, device_id=d, device_id_type=MESH)
    pl.semaphore_wait(sem, 9)

def merge(dst, own, other, core):
    a = own.astype(jnp.float32); b = other.astype(jnp.float32)
    first = jnp.where(core == 0, a, b); second = jnp.where(core == 0, b, a)
    return jnp.concatenate([first, second], axis=-2).astype(dst)

class GainRing:
    def __init__(self, g, ssem, rsem):
        self.g, self.ssem, self.rsem = g, ssem, rsem
        self.c, self.core = coords()
        self.sent = []

    def copy(self, f, s, right, origin):
        order = ORDERS[0]
        b = block(self.g, origin, order[:f])
        i = (f * 2 + s) * 2 + (0 if right else 1)
        return pltpu.make_async_remote_copy(
            src_ref=b, dst_ref=b, send_sem=self.ssem.at[i], recv_sem=self.rsem.at[i],
            device_id=device(moved(self.c, order[f], 1 if right else -1), self.core), device_id_type=MESH)

    def step(self, n):
        axes = ORDERS[0]
        if n > 0:
            f, s = (n - 1) // 2, (n - 1) % 2
            for right in (True, False) if s == 0 else (True,):
                self.copy(f, s, right, moved(self.c, axes[f], (1 + s) * (-1 if right else 1))).wait_recv()
        if n < 6:
            f, s = n // 2, n % 2
            for right in (True, False) if s == 0 else (True,):
                cp = self.copy(f, s, right, self.c if s == 0 else moved(self.c, axes[f], -1))
                cp.start()
                self.sent.append(cp)

    def finish(self):
        for cp in self.sent:
            cp.wait_send()


def gain_row(g):
    tiles = g[...].astype(F32).reshape(64, 8, 128)
    values = jnp.sum(tiles, axis=1).astype(BF)
    column = lax.broadcasted_iota(jnp.int32, (64, 1536), 1)
    chip = lax.broadcasted_iota(jnp.int32, (64, 1536), 0) * 24
    mine = jnp.where((column >= chip) & (column < chip + 24), 1.0, 0.0).astype(BF)
    spread = lax.dot_general(values, mine, (((0,), (0,)), ((), ())), preferred_element_type=F32)
    n = lax.broadcasted_iota(jnp.int32, (128, 1536), 1).astype(F32)
    within = n - 24.0 * jnp.floor((n + 0.5) * (1.0 / 24.0))
    j = lax.broadcasted_iota(jnp.int32, (128, 1536), 0).astype(F32)
    return jnp.sum(jnp.where(within == j, spread, 0.0), axis=0, keepdims=True)


def normalize(xb, nb, gain):
    def rows(start, size):
        wide = xb[pl.ds(start, size), :].astype(F32)
        factor = lax.rsqrt(jnp.mean(wide * wide, axis=-1, keepdims=True) + EPS)
        nb[pl.ds(start, size), :] = (wide * factor * gain).astype(BF)

    @pl.loop(0, 12)
    def _(i):
        rows(pl.multiple_of(i * 64, 64), 64)

    rows(768, 16)


def project(nb, w, u, t, lo, hi):
    @pl.loop(lo, hi)
    def _(j):
        rhs = w[t * 6 + j].reshape(1536, 256)
        u[:, pl.ds(pl.multiple_of(j * 256, 256), 256)] = jnp.dot(nb[...], rhs, preferred_element_type=F32)


def heads(u, cos, sin, qh, kh, vh, t):
    def turned(lo, half, r, c, s):
        a, b = u[r, lo : lo + half], u[r, lo + half : lo + 2 * half]
        return (a * c - b * s).astype(BF), (b * c + a * s).astype(BF)

    @pl.loop(0, 7)
    def _(i):
        r = pl.ds(pl.multiple_of(i * 112, 16), 112)
        c, s = cos[r, :], sin[r, :]
        a, b = turned(0, 384, r, c, s)
        for h in range(8):
            qh[8 * t + h, r, :] = jnp.concatenate([a[:, 48 * h : 48 * h + 48], b[:, 48 * h : 48 * h + 48]], axis=1)
        a, b = turned(768, 192, r, c[:, :192], s[:, :192])
        for h in range(4):
            kh[4 * t + h, r, :] = jnp.concatenate([a[:, 48 * h : 48 * h + 48], b[:, 48 * h : 48 * h + 48]], axis=1)
        for h in range(4):
            vh[4 * t + h, r, :] = u[r, 1152 + 96 * h : 1248 + 96 * h].astype(BF)


def attend(qh, kh, vh, attn, g):
    for i in range(3):
        lo, n = 256 * i, 256 * (i + 1)
        q = jnp.concatenate([qh[2 * g, lo:n, :], qh[2 * g + 1, lo:n, :]], axis=0)
        s = lax.dot_general(q, kh[g, 0:n, :], (((1,), (1,)), ((), ())), preferred_element_type=F32)
        row = lax.broadcasted_iota(jnp.int32, (512, 256), 0) & 255
        column = lax.broadcasted_iota(jnp.int32, (512, 256), 1)
        last = jnp.where(column <= row, s[:, lo:n], NEGATIVE)
        s = jnp.concatenate([s[:, :lo], last], axis=1) if i else last
        s = s * SCALE
        e = jnp.exp(s - jnp.max(s, axis=-1, keepdims=True))
        total = jnp.sum(e, axis=-1, keepdims=True)
        o = jnp.dot(e.astype(BF), vh[g, 0:n, :], preferred_element_type=F32)
        o = (o / total).astype(BF)
        attn[lo:n, 192 * g : 192 * g + 192] = jnp.concatenate([o[:256], o[256:]], axis=1)


def decode_block(qh, kc, vc, clen, pk, wide):
    q = qh[:, 768:784, :].astype(F32)
    lane = lax.broadcasted_iota(jnp.int32, (16, 768), 1)
    first = (lax.broadcasted_iota(jnp.int32, (16, 768), 0) // 2) * 96
    mine = (lane >= first) & (lane < first + 96)
    at = lax.axis_index("shard") * 512 + lax.broadcasted_iota(jnp.int32, (16, 512), 1)
    for r in range(8):
        one = q[:, r, :]
        spread = jnp.concatenate([one] * 8, axis=1)
        qw = jnp.where(mine, spread, 0.0).astype(BF)
        s = lax.dot_general(qw, kc[r], (((1,), (1,)), ((), ())), preferred_element_type=F32) * SCALE
        live = at < clen[r]
        s = jnp.where(live, s, NEGATIVE)
        peak = jnp.max(s, axis=-1, keepdims=True)
        e = jnp.where(live, jnp.exp(s - peak), 0.0)
        total = jnp.sum(e, axis=-1, keepdims=True)
        every = jnp.where(mine, jnp.dot(e.astype(BF), vc[r], preferred_element_type=F32), 0.0)
        acc = every[:, 0:96]
        for g in range(1, 8):
            acc = acc + every[:, 96 * g : 96 * g + 96]
        pk[:, r, :] = jnp.concatenate(
            [acc, jnp.broadcast_to(peak, (16, 16)), jnp.broadcast_to(total, (16, 16))], axis=1)


class Combine:
    def __init__(self, pk, rv, ssem, rsem):
        self.pk, self.rv, self.ssem, self.rsem = pk, rv, ssem, rsem
        self.sent = []

    def copy(self, j):
        c, core = coords()
        return pltpu.make_async_remote_copy(
            src_ref=self.pk.at[j], dst_ref=self.rv.at[j], send_sem=self.ssem.at[j], recv_sem=self.rsem.at[j],
            device_id=partner(c, core, j), device_id_type=MESH)

    def send(self, j):
        cp = self.copy(j)
        cp.start()
        self.sent.append(cp)

    def add(self, j):
        self.copy(j).wait_recv()
        a, b = self.pk[j], self.rv[j]
        pa, pb = a[:, :, 96:97], b[:, :, 96:97]
        top = jnp.maximum(pa, pb)
        both = a * jnp.exp(pa - top) + b * jnp.exp(pb - top)
        lane = lax.broadcasted_iota(jnp.int32, both.shape, 2)
        self.pk[j + 1] = jnp.where((lane >= 96) & (lane < 112), top, both)

    def finish(self):
        for cp in self.sent:
            cp.wait_send()


def partner(c, core, j):
    if j == 0:
        return device(c, 1 - core)
    if j == 1:
        return device(moved(c, "y", 2), core)
    if j == 2:
        return device({**c, "x": c["x"] + 1 - 2 * (c["x"] % 2)}, core)
    return device(moved(c, "x", 2), core)


def decode_mix(pk, qh, kh, vh, attn):
    a = pk[4]
    acc, peak, total = a[:, :, 0:96], a[:, :, 96:97], a[:, :, 112:113]

    def pairs(ref):
        v = ref[:, 768:784, :].astype(F32)[:, 0:8, :]
        return jnp.broadcast_to(v[:, None], (8, 2, 8, 96)).reshape(16, 8, 96)

    q = qh[:, 768:784, :].astype(F32)[:, 0:8, :]
    own = jnp.sum(q * pairs(kh), axis=-1, keepdims=True) * SCALE
    top = jnp.maximum(peak, own)
    old, new = jnp.exp(peak - top), jnp.exp(own - top)
    mix = (acc * old + new * pairs(vh)) / (total * old + new)
    zero = jnp.zeros((8, 96), F32)
    for h in range(16):
        attn[768:784, 96 * h : 96 * h + 96] = jnp.concatenate([mix[h], zero], axis=0).astype(BF)


def kernel(slab_ref, gain_ref, x_ref, dx_ref, cos, sin, k_ref, v_ref, clen, out_ref, dout_ref,
           own, other, gown, gother, w, g, xb, nb, u, qh, kh, vh, attn, kc, vc, o, pk, rv,
           ssem, rsem, ds, dr, ps, pr, gs, gr, cs, cr, lsem, osem):
    c, core = coords()
    loads = [pltpu.make_async_copy(s, d, lsem.at[i]) for i, (s, d) in enumerate((
        (slab_ref, own), (gain_ref, gown), (x_ref, xb.at[pl.ds(0, 768)]), (dx_ref, xb.at[pl.ds(768, 16)]),
        (k_ref, kc), (v_ref, vc)))]
    for cp in loads[:2]:
        cp.start()
    barrier(c, core)
    for cp in loads[:2]:
        cp.wait()
    pre = [pltpu.make_async_remote_copy(
        src_ref=s, dst_ref=d, send_sem=ps.at[i], recv_sem=pr.at[i],
        device_id=device(c, 1 - core), device_id_type=MESH)
        for i, (s, d) in enumerate(((own.at[1 - core], other), (gown, gother)))]
    for cp in pre:
        cp.start()
    for cp in loads[2:]:
        cp.start()
    for cp in pre:
        cp.wait()
    for i in range(3 * N_CHUNK):
        t, k = i // 3, i % 3
        w[t * 6 + core * 3 + k, c["z"], c["y"] % 2, c["x"], c["y"] // 2] = merge(BF, own[core, i], other[i], core)
    g[c["z"], c["y"] % 2, c["x"], c["y"] // 2] = (gown[...].astype(F32) + gother[...].astype(F32)).astype(BF)
    G = Gather(w, ssem, rsem, ds, dr)
    R = GainRing(g, gs, gr)
    D = Combine(pk, rv, cs, cr)

    for tick in range(5):
        R.step(tick)
        for t in range(N_CHUNK):
            if 0 <= tick - LAG * t <= 6:
                G.step(t, tick - LAG * t)
    R.step(5)
    R.step(6)
    for cp in loads[2:4]:
        cp.wait()
    normalize(xb, nb, gain_row(g))
    G.step(0, 5)
    G.step(1, 3)
    G.step(2, 1)
    G.step(0, 6)
    G.step(1, 4)
    G.step(2, 2)
    G.take(0)
    project(nb, w, u, 0, 0, 3)
    G.step(2, 3)
    project(nb, w, u, 0, 3, 6)
    G.step(1, 5)
    heads(u, cos, sin, qh, kh, vh, 0)
    G.step(1, 6)
    G.step(2, 4)
    attend(qh, kh, vh, attn, 0)
    attend(qh, kh, vh, attn, 1)
    G.step(2, 5)
    attend(qh, kh, vh, attn, 2)
    attend(qh, kh, vh, attn, 3)
    G.step(2, 6)
    G.take(1)
    project(nb, w, u, 1, 0, 6)
    heads(u, cos, sin, qh, kh, vh, 1)
    for cp in loads[4:]:
        cp.wait()
    decode_block(qh, kc, vc, clen, pk.at[0], None)
    for j in range(4):
        D.send(j)
        attend(qh, kh, vh, attn, 4 + j)
        D.add(j)
    decode_mix(pk, qh, kh, vh, attn)
    G.take(2)

    @pl.loop(0, 6)
    def _(j):
        rhs = w[12 + j].reshape(1536, 256)
        o[:, pl.ds(pl.multiple_of(j * 256, 256), 256)] = jnp.dot(
            attn[...], rhs, preferred_element_type=F32).astype(BF)

    outs = [pltpu.make_async_copy(o.at[pl.ds(0, 768)], out_ref, osem.at[0]),
            pltpu.make_async_copy(o.at[pl.ds(768, 16)], dout_ref, osem.at[1])]
    for cp in outs:
        cp.start()
    G.finish()
    R.finish()
    D.finish()
    for cp in outs:
        cp.wait()


LAG = 2


def per_device(prefill_x, decode_x, norm_gain, wqkv, wo, k_cache, v_cache, cache_len):
    q = wqkv[:, :1536].reshape(12, 2, 8, 2, 48).transpose(1, 0, 3, 2, 4).reshape(2, 12, 768)
    k = wqkv[:, 1536:2304].reshape(12, 2, 4, 2, 48).transpose(1, 0, 3, 2, 4).reshape(2, 12, 384)
    v = wqkv[:, 2304:].reshape(12, 2, 384).transpose(1, 0, 2)
    chunks = jnp.concatenate([jnp.concatenate([q, k, v], axis=2), wo[None]], axis=0)
    slab = chunks.reshape(3, 12, 2, 3, 256).transpose(2, 0, 3, 1, 4).reshape(2, 9, 12, 256)
    core = lax.axis_index("shard") % 2
    row = jnp.concatenate([jnp.where(core == 0, norm_gain, 0), jnp.where(core == 1, norm_gain, 0)])
    gain_tile = jnp.pad(row[None], ((0, 7), (0, 104)))
    frequency = jnp.power(THETA, -jnp.arange(48, dtype=F32) * (2.0 / HD))
    positions = jnp.concatenate([jnp.arange(768, dtype=jnp.int32), cache_len, jnp.zeros((8,), jnp.int32)])
    angles = positions.astype(F32)[:, None] * frequency[None, :]
    cos = jnp.tile(jnp.cos(angles), (1, 8))
    sin = jnp.tile(jnp.sin(angles), (1, 8))
    dx = jnp.concatenate([decode_x, jnp.zeros((8, 1536), BF)], axis=0)
    hbm, vmem = pl.BlockSpec(memory_space=pl.ANY), pl.BlockSpec(memory_space=pltpu.VMEM)
    n = N_CHUNK
    dma = pltpu.SemaphoreType.DMA
    out, dout = pl.pallas_call(
        kernel,
        out_shape=(jax.ShapeDtypeStruct((768, 1536), BF), jax.ShapeDtypeStruct((16, 1536), BF)),
        in_specs=[hbm, hbm, hbm, hbm, vmem, vmem, hbm, hbm, pl.BlockSpec(memory_space=pltpu.SMEM)],
        out_specs=(hbm, hbm),
        scratch_shapes=[
            pltpu.VMEM((2, 3 * n, 12, 256), BF), pltpu.VMEM((3 * n, 12, 256), BF),
            pltpu.VMEM((8, 128), BF), pltpu.VMEM((8, 128), BF),
            pltpu.VMEM((6 * n, 4, 2, 4, 2, 24, 256), BF), pltpu.VMEM((4, 2, 4, 2, 8, 128), BF),
            pltpu.VMEM((784, 1536), BF), pltpu.VMEM((784, 1536), BF), pltpu.VMEM((784, 1536), F32),
            pltpu.VMEM((16, 784, 96), BF), pltpu.VMEM((8, 784, 96), BF), pltpu.VMEM((8, 784, 96), BF),
            pltpu.VMEM((784, 1536), BF), pltpu.VMEM((8, 512, 768), BF), pltpu.VMEM((8, 512, 768), BF),
            pltpu.VMEM((784, 1536), BF), pltpu.VMEM((5, 16, 8, 128), F32), pltpu.VMEM((4, 16, 8, 128), F32),
            dma((36 * n,)), dma((36 * n,)), dma((12 * n,)), dma((12 * n,)), dma((2,)), dma((2,)),
            dma((12,)), dma((12,)), dma((4,)), dma((4,)), dma((6,)), dma((2,)),
        ],
        compiler_params=pltpu.CompilerParams(
            collective_id=0, has_side_effects=True, vmem_limit_bytes=67043328),
        name="sublayer",
    )(slab, gain_tile, prefill_x, dx, cos, sin, k_cache, v_cache, cache_len)
    return out, dout[:8]


def solution(mesh):
    rows = P(("dp", "shard"), None)
    in_specs = (rows, P("dp", None), P(("dp", "shard")), rows, rows,
                P("dp", "shard", None), P("dp", "shard", None), P("dp"))
    return jax.shard_map(per_device, mesh=mesh, in_specs=in_specs,
                         out_specs=(rows, P("dp", None)), check_vma=False)
```

time: 698 us -> 114 us (0.16)
  waiting for transfers between devices: 316 us -> 0 us
  blocking collectives: 201 us -> 0 us
  Pallas kernels: 0 us -> 97.2 us
  matrix products: 96.6 us -> 0 us
  local copies, waits for them, and re-layouts: 58.2 us -> 13.3 us
  between operations: 14.2 us -> 0.73 us
  other arithmetic: 9.72 us -> 2.32 us
    all_gather x2 -> x0, waiting for transfers between devices: 315 us -> none  [the longest x1 199 us: per_device(): weight_rows = lax.all_gather(wqkv, ('dp', 'shard'), axis=0, tiled=True)]
    pallas_call x0 -> x1, Pallas kernels: none -> 97.2 us  [per_device(): pl.pallas_call(kernel, out_shape=(jax.ShapeDtypeStruct((768, 1536), BF),...]
    unnamed x1 -> x0, blocking collectives: 68.3 us -> none
    pmax x1 -> x0, blocking collectives: 67.2 us -> none  [per_device(): group_top = lax.pmax(block_peaks, 'shard')]
    psum x1 -> x0, blocking collectives: 65.7 us -> none  [per_device(): lax.psum((partial_sums * rescale[..., None], partial_totals * rescale), '...]
    dot_general x13 -> x0, matrix products: 57.2 us -> none  [the longest x8 29.3 us: one_head(): jnp.einsum('gqs,sd->qgd', weights, value_head, preferred_element_type=jnp...]
    sub x8 -> x0, matrix products: 39.4 us -> none  [one_head(): expanded = jnp.exp(scores - highest)]
    unnamed x12 -> x1, local copies, waits for them, and re-layouts: 40.2 us -> 3.22 us
  transfers between devices with their start and end apart: 2 -> 0, of which waited for: 2 -> 0; matrix products, arithmetic and copies ran while one was open for 4% -> 0% of each run, Pallas kernels for 0% -> 0%
where the time goes in v1:
time: 114 us
  Pallas kernels  97.2 us (85%)
  local copies, waits for them, and re-layouts  13.3 us (12%)
  other arithmetic  2.32 us (2%)
    pallas_call x1, Pallas kernels, per_device(): pl.pallas_call(kernel, out_shape=(jax.ShapeDtypeStruct((768, 1536), BF),...  97.2 us
    unnamed x1, local copies, waits for them, and re-layouts  3.22 us

profile of v1, /device:TPU:0, one launch (start us, length us, event | category | flops | bytes accessed | tf_op | source)
XLA Modules:
  0.0 113.5 jit_solution(3862721032519545586)
XLA Ops:
  0.6 0.7 broadcast_select_fusion.1
  1.3 0.1 maximum_bitcast_fusion.1
  1.4 0.6 pad.5.gain_ref
  2.0 0.7 add_convert_fusion
  2.7 1.4 %concatenate.31.dx_ref = bf16[16,1536]{1,0:T(8,128)(2,1)} pad(bf16[8,1536]{1,0:T(8,128)(2,1)} %param.9, bf16[]{:T(256)} %constant.24.clone.1), padding=0_8x0_0 | pad | bytes 73730 | tf_op jit(solution)/shard_map/concatenate | solution.py:415
  4.1 0.8 concatenate.28
  4.9 0.8 slice.12
  5.7 0.1 reshape.107
  5.9 0.2 reshape.108
  6.0 0.8 fusion
  6.8 0.1 reshape.109
  7.0 0.1 reshape.110
  7.1 0.1 pad_maximum_fusion
  7.2 0.1 concatenate.27
  7.2 0.1 maximum_bitcast_fusion
  7.3 0.7 copy.15
  8.0 0.7 multiply_sine_fusion
  8.7 0.1 tile.20
  8.8 1.4 %copy.17.sin = f32[784,384]{1,0:T(8,128)} copy(f32[784,384]{0,1:T(8,128)S(1)} %bitcast.23) | data formatting | bytes 2408448 | tf_op jit(solution)/shard_map/tile | solution.py:414
  10.2 0.1 tile.8
  10.3 1.4 %copy.16.cos = f32[784,384]{1,0:T(8,128)} copy(f32[784,384]{0,1:T(8,128)S(1)} %bitcast.24) | data formatting | bytes 2408448 | tf_op jit(solution)/shard_map/tile | solution.py:413
  11.7 97.2 %sublayer.1 = (bf16[768,1536]{1,0:T(8,128)(2,1)}, bf16[16,1536]{1,0:T(8,128)(2,1)}) custom-call(bf16[2,9,12,256]{3,2,1,0:T(8,128)(2,1)} %bitcast.25, bf16[8,128]{1,0:T(8,128)(2,1)} %pad.5.gain_ref, bf16[768,1536]{1,0:T(8,128)(2,1)} %x_ref.1, bf16[16,1536]{1,0:T(8,128)(2,1)} %concatenate.31.dx_ref, f32[784,384]{1,0:T(8,128)} %copy.16.cos, ...), custom_call_target="tpu_custom_call" | custom-call | tf_op jit(solution)/shard_map/sublayer/pallas_call | solution.py:419
  109.0 1.3 %slice.15 = bf16[8,1536]{1,0:T(8,128)(2,1)} slice(bf16[16,1536]{1,0:T(8,128)(2,1)} %get-tuple-element.5), slice={[0:8], [0:1536]} | slice | bytes 49152 | tf_op jit(solution)/shard_map/slice | solution.py:439
  110.3 3.2 %copy.23 = bf16[768,1536]{1,0:T(8,128)(2,1)} copy(bf16[768,1536]{1,0:T(8,128)(2,1)} %get-tuple-element.14) | data formatting | bytes 4718592
  (6 shorter events, 0.1 us)

commit v2 on v1

--- a/solution.py
+++ b/solution.py
@@ -1,5 +1,6 @@
 import jax
 import jax.numpy as jnp
+import numpy as np
 from jax import lax
 from jax.experimental import pallas as pl
 from jax.experimental.pallas import tpu as pltpu
@@ -117,10 +118,51 @@
         pl.semaphore_signal(sem, inc=1, device_id=d, device_id_type=MESH)
     pl.semaphore_wait(sem, 9)
 
-def merge(dst, own, other, core):
-    a = own.astype(jnp.float32); b = other.astype(jnp.float32)
-    first = jnp.where(core == 0, a, b); second = jnp.where(core == 0, b, a)
-    return jnp.concatenate([first, second], axis=-2).astype(dst)
+def both_rows(own, other, core):
+    a, b = own[...].astype(F32), other[...].astype(F32)
+    return jnp.concatenate([jnp.where(core == 0, a, b), jnp.where(core == 0, b, a)], axis=0)
+
+
+def merge(t, own_q, other_q, own_o, other_o, w, c, core):
+    if t == 2:
+        cols = both_rows(own_o, other_o, core)
+    else:
+        a = both_rows(own_q, other_q, core)
+        starts = [96 * (8 * t + h) + 48 * half for half in range(2) for h in range(8)]
+        starts += [1536 + 96 * (4 * t + h) + 48 * half for half in range(2) for h in range(4)]
+        v = 2304 + 384 * t
+        cols = jnp.concatenate([a[:, n : n + 48] for n in starts] + [a[:, v : v + 384]], axis=1)
+    for k in range(3):
+        part = jnp.where(core == 0, cols[:, 256 * k : 256 * k + 256], cols[:, 768 + 256 * k : 1024 + 256 * k])
+        w[t * 6 + core * 3 + k, c["z"], c["y"] % 2, c["x"], c["y"] // 2] = part.astype(BF)
+
+
+def gain_tile(gain, core):
+    g = gain[...].astype(F32)
+    zero = jnp.zeros((1, 116), F32)
+    row = jnp.where(core == 0, jnp.concatenate([g, zero], axis=1),
+                    jnp.concatenate([zero[:, :12], g, zero[:, :104]], axis=1))
+    first = lax.broadcasted_iota(jnp.int32, (8, 128), 0) == 0
+    return jnp.where(first, jnp.broadcast_to(row, (8, 128)), 0.0).astype(BF)
+
+
+def angles(freq, clen, cos, sin):
+    def put(start, size, at):
+        a = at.astype(F32) * freq[...]
+        rows = pl.ds(start, size)
+        cos[rows, :] = jnp.concatenate([jnp.cos(a)[:, :48]] * 8, axis=1)
+        sin[rows, :] = jnp.concatenate([jnp.sin(a)[:, :48]] * 8, axis=1)
+
+    @pl.loop(0, 16)
+    def _(i):
+        put(pl.multiple_of(i * 48, 16), 48, lax.broadcasted_iota(jnp.int32, (48, 128), 0) + i * 48)
+
+    row = lax.broadcasted_iota(jnp.int32, (16, 128), 0)
+    at = jnp.zeros((16, 128), jnp.int32)
+    for r in range(8):
+        at = jnp.where(row == r, clen[r], at)
+    put(768, 16, at)
+
 
 class GainRing:
     def __init__(self, g, ssem, rsem):
@@ -168,16 +210,17 @@
 
 
 def normalize(xb, nb, gain):
-    def rows(start, size):
+    def scaled(start, size):
         wide = xb[pl.ds(start, size), :].astype(F32)
         factor = lax.rsqrt(jnp.mean(wide * wide, axis=-1, keepdims=True) + EPS)
-        nb[pl.ds(start, size), :] = (wide * factor * gain).astype(BF)
+        return wide * factor * gain
 
     @pl.loop(0, 12)
     def _(i):
-        rows(pl.multiple_of(i * 64, 64), 64)
-
-    rows(768, 16)
+        start = pl.multiple_of(i * 64, 64)
+        nb[pl.ds(start, 64), :] = scaled(start, 64).astype(BF)
+
+    nb[768:784, :] = jnp.concatenate([scaled(768, 8), jnp.zeros((8, 1536), F32)], axis=0).astype(BF)
 
 
 def project(nb, w, u, t, lo, hi):
@@ -305,31 +348,29 @@
         attn[768:784, 96 * h : 96 * h + 96] = jnp.concatenate([mix[h], zero], axis=0).astype(BF)
 
 
-def kernel(slab_ref, gain_ref, x_ref, dx_ref, cos, sin, k_ref, v_ref, clen, out_ref, dout_ref,
-           own, other, gown, gother, w, g, xb, nb, u, qh, kh, vh, attn, kc, vc, o, pk, rv,
+def kernel(wq_ref, wo_ref, gain_ref, x_ref, dx_ref, freq, k_ref, v_ref, clen, out_ref, dout_ref,
+           own_q, own_o, other_q, other_o, gown, gother, w, g, xb, nb, u, cos, sin, qh, kh, vh, attn, kc, vc, o, pk, rv,
            ssem, rsem, ds, dr, ps, pr, gs, gr, cs, cr, lsem, osem):
     c, core = coords()
     loads = [pltpu.make_async_copy(s, d, lsem.at[i]) for i, (s, d) in enumerate((
-        (slab_ref, own), (gain_ref, gown), (x_ref, xb.at[pl.ds(0, 768)]), (dx_ref, xb.at[pl.ds(768, 16)]),
+        (wq_ref, own_q), (wo_ref, own_o), (x_ref, xb.at[pl.ds(0, 768)]), (dx_ref, xb.at[pl.ds(768, 8)]),
         (k_ref, kc), (v_ref, vc)))]
     for cp in loads[:2]:
         cp.start()
+    gown[...] = gain_tile(gain_ref, core)
     barrier(c, core)
-    for cp in loads[:2]:
-        cp.wait()
     pre = [pltpu.make_async_remote_copy(
         src_ref=s, dst_ref=d, send_sem=ps.at[i], recv_sem=pr.at[i],
         device_id=device(c, 1 - core), device_id_type=MESH)
-        for i, (s, d) in enumerate(((own.at[1 - core], other), (gown, gother)))]
+        for i, (s, d) in enumerate(((wq_ref, other_q), (wo_ref, other_o), (gown, gother)))]
     for cp in pre:
         cp.start()
     for cp in loads[2:]:
         cp.start()
+    for cp in loads[:2]:
+        cp.wait()
     for cp in pre:
         cp.wait()
-    for i in range(3 * N_CHUNK):
-        t, k = i // 3, i % 3
-        w[t * 6 + core * 3 + k, c["z"], c["y"] % 2, c["x"], c["y"] // 2] = merge(BF, own[core, i], other[i], core)
     g[c["z"], c["y"] % 2, c["x"], c["y"] // 2] = (gown[...].astype(F32) + gother[...].astype(F32)).astype(BF)
     G = Gather(w, ssem, rsem, ds, dr)
     R = GainRing(g, gs, gr)
@@ -338,9 +379,12 @@
     for tick in range(5):
         R.step(tick)
         for t in range(N_CHUNK):
+            if tick == LAG * t:
+                merge(t, own_q, other_q, own_o, other_o, w, c, core)
             if 0 <= tick - LAG * t <= 6:
                 G.step(t, tick - LAG * t)
     R.step(5)
+    angles(freq, clen, cos, sin)
     R.step(6)
     for cp in loads[2:4]:
         cp.wait()
@@ -378,16 +422,20 @@
     decode_mix(pk, qh, kh, vh, attn)
     G.take(2)
 
+    def leaving(j):
+        cols = pl.ds(pl.multiple_of(j * 256, 256), 256)
+        return pltpu.make_async_copy(o.at[pl.ds(0, 768), cols], out_ref.at[:, cols], osem.at[j])
+
     @pl.loop(0, 6)
     def _(j):
         rhs = w[12 + j].reshape(1536, 256)
         o[:, pl.ds(pl.multiple_of(j * 256, 256), 256)] = jnp.dot(
             attn[...], rhs, preferred_element_type=F32).astype(BF)
-
-    outs = [pltpu.make_async_copy(o.at[pl.ds(0, 768)], out_ref, osem.at[0]),
-            pltpu.make_async_copy(o.at[pl.ds(768, 16)], dout_ref, osem.at[1])]
-    for cp in outs:
-        cp.start()
+        leaving(j).start()
+
+    outs = [leaving(j) for j in range(6)]
+    outs.append(pltpu.make_async_copy(o.at[pl.ds(768, 8)], dout_ref, osem.at[6]))
+    outs[6].start()
     G.finish()
     R.finish()
     D.finish()
@@ -399,44 +447,33 @@
 
 
 def per_device(prefill_x, decode_x, norm_gain, wqkv, wo, k_cache, v_cache, cache_len):
-    q = wqkv[:, :1536].reshape(12, 2, 8, 2, 48).transpose(1, 0, 3, 2, 4).reshape(2, 12, 768)
-    k = wqkv[:, 1536:2304].reshape(12, 2, 4, 2, 48).transpose(1, 0, 3, 2, 4).reshape(2, 12, 384)
-    v = wqkv[:, 2304:].reshape(12, 2, 384).transpose(1, 0, 2)
-    chunks = jnp.concatenate([jnp.concatenate([q, k, v], axis=2), wo[None]], axis=0)
-    slab = chunks.reshape(3, 12, 2, 3, 256).transpose(2, 0, 3, 1, 4).reshape(2, 9, 12, 256)
-    core = lax.axis_index("shard") % 2
-    row = jnp.concatenate([jnp.where(core == 0, norm_gain, 0), jnp.where(core == 1, norm_gain, 0)])
-    gain_tile = jnp.pad(row[None], ((0, 7), (0, 104)))
-    frequency = jnp.power(THETA, -jnp.arange(48, dtype=F32) * (2.0 / HD))
-    positions = jnp.concatenate([jnp.arange(768, dtype=jnp.int32), cache_len, jnp.zeros((8,), jnp.int32)])
-    angles = positions.astype(F32)[:, None] * frequency[None, :]
-    cos = jnp.tile(jnp.cos(angles), (1, 8))
-    sin = jnp.tile(jnp.sin(angles), (1, 8))
-    dx = jnp.concatenate([decode_x, jnp.zeros((8, 1536), BF)], axis=0)
+    freq = np.power(np.float32(THETA), -np.arange(48, dtype=np.float32) * np.float32(2.0 / HD))
+    freq = jnp.asarray(np.pad(freq.astype(np.float32)[None], ((0, 0), (0, 80))))
     hbm, vmem = pl.BlockSpec(memory_space=pl.ANY), pl.BlockSpec(memory_space=pltpu.VMEM)
     n = N_CHUNK
     dma = pltpu.SemaphoreType.DMA
     out, dout = pl.pallas_call(
         kernel,
-        out_shape=(jax.ShapeDtypeStruct((768, 1536), BF), jax.ShapeDtypeStruct((16, 1536), BF)),
-        in_specs=[hbm, hbm, hbm, hbm, vmem, vmem, hbm, hbm, pl.BlockSpec(memory_space=pltpu.SMEM)],
+        out_shape=(jax.ShapeDtypeStruct((768, 1536), BF), jax.ShapeDtypeStruct((8, 1536), BF)),
+        in_specs=[hbm, hbm, vmem, hbm, hbm, vmem, hbm, hbm, pl.BlockSpec(memory_space=pltpu.SMEM)],
         out_specs=(hbm, hbm),
         scratch_shapes=[
-            pltpu.VMEM((2, 3 * n, 12, 256), BF), pltpu.VMEM((3 * n, 12, 256), BF),
+            pltpu.VMEM((12, 3072), BF), pltpu.VMEM((12, 1536), BF), pltpu.VMEM((12, 3072), BF), pltpu.VMEM((12, 1536), BF),
             pltpu.VMEM((8, 128), BF), pltpu.VMEM((8, 128), BF),
             pltpu.VMEM((6 * n, 4, 2, 4, 2, 24, 256), BF), pltpu.VMEM((4, 2, 4, 2, 8, 128), BF),
             pltpu.VMEM((784, 1536), BF), pltpu.VMEM((784, 1536), BF), pltpu.VMEM((784, 1536), F32),
+            pltpu.VMEM((784, 384), F32), pltpu.VMEM((784, 384), F32),
             pltpu.VMEM((16, 784, 96), BF), pltpu.VMEM((8, 784, 96), BF), pltpu.VMEM((8, 784, 96), BF),
             pltpu.VMEM((784, 1536), BF), pltpu.VMEM((8, 512, 768), BF), pltpu.VMEM((8, 512, 768), BF),
             pltpu.VMEM((784, 1536), BF), pltpu.VMEM((5, 16, 8, 128), F32), pltpu.VMEM((4, 16, 8, 128), F32),
-            dma((36 * n,)), dma((36 * n,)), dma((12 * n,)), dma((12 * n,)), dma((2,)), dma((2,)),
-            dma((12,)), dma((12,)), dma((4,)), dma((4,)), dma((6,)), dma((2,)),
+            dma((36 * n,)), dma((36 * n,)), dma((12 * n,)), dma((12 * n,)), dma((3,)), dma((3,)),
+            dma((12,)), dma((12,)), dma((4,)), dma((4,)), dma((6,)), dma((7,)),
         ],
         compiler_params=pltpu.CompilerParams(
             collective_id=0, has_side_effects=True, vmem_limit_bytes=67043328),
         name="sublayer",
-    )(slab, gain_tile, prefill_x, dx, cos, sin, k_cache, v_cache, cache_len)
-    return out, dout[:8]
+    )(wqkv, wo, norm_gain.reshape(1, 12), prefill_x, decode_x, freq, k_cache, v_cache, cache_len)
+    return out, dout
 
 
 def solution(mesh):

time: 114 us -> 101 us (0.89)
  local copies, waits for them, and re-layouts: 13.3 us -> 3.84 us
  other arithmetic: 2.32 us -> 0 us
  Pallas kernels: 97.2 us -> 95.8 us
    another operation x4 -> x0, local copies, waits for them, and re-layouts: 3.05 us -> none  [the longest x2 1.54 us: per_device(): sin = jnp.tile(jnp.sin(angles), (1, 8))]
    slice x3 -> x0, local copies, waits for them, and re-layouts: 2.92 us -> none  [the longest x1 1.35 us: per_device(): return (out, dout[:8])]
    concatenate x4 -> x0, local copies, waits for them, and re-layouts: 2.24 us -> none  [the longest x1 1.35 us: per_device(): dx = jnp.concatenate([decode_x, jnp.zeros((8, 1536), BF)], axis=0)]
    pallas_call x1, Pallas kernels: 97.2 us -> 95.8 us  [per_device(): pl.pallas_call(kernel, out_shape=(jax.ShapeDtypeStruct((768, 1536), BF),...]
    unnamed x1 -> x4, local copies, waits for them, and re-layouts: 3.22 us -> 3.84 us
where the time goes in v2:
time: 101 us; the launch traced here: 100 us
  Pallas kernels  95.8 us (95%)
  local copies, waits for them, and re-layouts  3.84 us (4%)
    pallas_call x1, Pallas kernels, per_device(): pl.pallas_call(kernel, out_shape=(jax.ShapeDtypeStruct((768, 1536), BF),...  95.8 us
    unnamed x4, local copies, waits for them, and re-layouts  3.84 us

profile of v2, /device:TPU:0, one launch (start us, length us, event | category | flops | bytes accessed | tf_op | source)
XLA Modules:
  0.0 100.3 jit_solution(13705642812706403343)
XLA Ops:
  0.6 95.8 %sublayer.1 = (bf16[768,1536]{1,0:T(8,128)(2,1)}, bf16[8,1536]{1,0:T(8,128)(2,1)}) custom-call(bf16[12,3072]{1,0:T(8,128)(2,1)} %wq_ref.1, bf16[12,1536]{1,0:T(8,128)(2,1)} %wo_ref.1, bf16[1,12]{1,0:T(2,128)(2,1)} %bitcast.1, bf16[768,1536]{1,0:T(8,128)(2,1)} %x_ref.1, bf16[8,1536]{1,0:T(8,128)(2,1)} %dx_ref.1, f32[1,128]{1,0:T(1,128)} %constant.2.clone.freq, ...), custom_call_target="tpu_custom_call" | custom-call | tf_op jit(solution)/shard_map/sublayer/pallas_call | solution.py:455
  96.4 0.0 copy-start
  96.4 3.2 %copy.13 = bf16[768,1536]{1,0:T(8,128)(2,1)} copy(bf16[768,1536]{1,0:T(8,128)(2,1)} %get-tuple-element.4) | data formatting | bytes 4718592
  99.7 0.0 copy-done
  99.7 0.6 copy.14
Async XLA Ops:
  96.4 3.2 %copy-start = (bf16[8,1536]{1,0:T(8,128)(2,1)S(1)}, bf16[8,1536]{1,0:T(8,128)(2,1)}, u32[]{:S(2)}) copy-start(bf16[8,1536]{1,0:T(8,128)(2,1)} %get-tuple-element.5) | copy-start | bytes 73732

commit v3 on v2

--- a/solution.py
+++ b/solution.py
@@ -128,7 +128,7 @@
         cols = both_rows(own_o, other_o, core)
     else:
         a = both_rows(own_q, other_q, core)
-        starts = [96 * (8 * t + h) + 48 * half for half in range(2) for h in range(8)]
+        starts = [96 * (8 * t + 2 * g + e) + 48 * half for half in range(2) for e in range(2) for g in range(4)]
         starts += [1536 + 96 * (4 * t + h) + 48 * half for half in range(2) for h in range(4)]
         v = 2304 + 384 * t
         cols = jnp.concatenate([a[:, n : n + 48] for n in starts] + [a[:, v : v + 384]], axis=1)
@@ -230,30 +230,38 @@
         u[:, pl.ds(pl.multiple_of(j * 256, 256), 256)] = jnp.dot(nb[...], rhs, preferred_element_type=F32)
 
 
-def heads(u, cos, sin, qh, kh, vh, t):
+def heads(u, cos, sin, qe, qo, kp, vp, t):
     def turned(lo, half, r, c, s):
         a, b = u[r, lo : lo + half], u[r, lo + half : lo + 2 * half]
         return (a * c - b * s).astype(BF), (b * c + a * s).astype(BF)
+
+    def packed(a, b, lo):
+        return jnp.concatenate([a[:, lo : lo + 96], b[:, lo : lo + 96], a[:, lo + 96 : lo + 192], b[:, lo + 96 : lo + 192]], axis=1)
 
     @pl.loop(0, 7)
     def _(i):
         r = pl.ds(pl.multiple_of(i * 112, 16), 112)
         c, s = cos[r, :], sin[r, :]
         a, b = turned(0, 384, r, c, s)
-        for h in range(8):
-            qh[8 * t + h, r, :] = jnp.concatenate([a[:, 48 * h : 48 * h + 48], b[:, 48 * h : 48 * h + 48]], axis=1)
+        qe[t, r, :] = packed(a, b, 0)
+        qo[t, r, :] = packed(a, b, 192)
         a, b = turned(768, 192, r, c[:, :192], s[:, :192])
-        for h in range(4):
-            kh[4 * t + h, r, :] = jnp.concatenate([a[:, 48 * h : 48 * h + 48], b[:, 48 * h : 48 * h + 48]], axis=1)
-        for h in range(4):
-            vh[4 * t + h, r, :] = u[r, 1152 + 96 * h : 1248 + 96 * h].astype(BF)
-
-
-def attend(qh, kh, vh, attn, g):
+        kp[t, r, :] = packed(a, b, 0)
+        vp[t, r, :] = u[r, 1152:1536].astype(BF)
+
+
+def attend(qe, qo, kp, vp, attn, g):
+    t, pair, j = g // 4, g % 4 // 2, g % 2
+    win = slice(128 * pair, 128 * pair + 256)
+    base = 64 * pair + 48 * j
+    lane = lax.broadcasted_iota(jnp.int32, (16, 256), 1)
+    mine = ((lane >= base) & (lane < base + 48)) | ((lane >= base + 96) & (lane < base + 144))
+    mine = jnp.where(mine, 1.0, 0.0).astype(BF)[:1]
+    off = 96 * (g % 4) - 128 * pair
     for i in range(3):
         lo, n = 256 * i, 256 * (i + 1)
-        q = jnp.concatenate([qh[2 * g, lo:n, :], qh[2 * g + 1, lo:n, :]], axis=0)
-        s = lax.dot_general(q, kh[g, 0:n, :], (((1,), (1,)), ((), ())), preferred_element_type=F32)
+        q = jnp.concatenate([qe[t, lo:n, win] * mine, qo[t, lo:n, win] * mine], axis=0)
+        s = lax.dot_general(q, kp[t, 0:n, win], (((1,), (1,)), ((), ())), preferred_element_type=F32)
         row = lax.broadcasted_iota(jnp.int32, (512, 256), 0) & 255
         column = lax.broadcasted_iota(jnp.int32, (512, 256), 1)
         last = jnp.where(column <= row, s[:, lo:n], NEGATIVE)
@@ -261,13 +269,23 @@
         s = s * SCALE
         e = jnp.exp(s - jnp.max(s, axis=-1, keepdims=True))
         total = jnp.sum(e, axis=-1, keepdims=True)
-        o = jnp.dot(e.astype(BF), vh[g, 0:n, :], preferred_element_type=F32)
-        o = (o / total).astype(BF)
+        o = jnp.dot(e.astype(BF), vp[t, 0:n, win], preferred_element_type=F32)
+        o = (o * (1.0 / total)).astype(BF)[:, off : off + 96]
         attn[lo:n, 192 * g : 192 * g + 192] = jnp.concatenate([o[:256], o[256:]], axis=1)
 
 
-def decode_block(qh, kc, vc, clen, pk, wide):
-    q = qh[:, 768:784, :].astype(F32)
+def decode_rows(ref, t, g):
+    lo = 192 * (g // 2) + 48 * (g % 2)
+    rows = jnp.concatenate([ref[t, 768:784, lo : lo + 48], ref[t, 768:784, lo + 96 : lo + 144]], axis=1)
+    return rows.astype(F32)[:8]
+
+
+def decode_queries(qe, qo):
+    return jnp.stack([decode_rows((qe, qo)[h % 2], h // 8, h % 8 // 2) for h in range(16)])
+
+
+def decode_block(qe, qo, kc, vc, clen, pk):
+    q = decode_queries(qe, qo)
     lane = lax.broadcasted_iota(jnp.int32, (16, 768), 1)
     first = (lax.broadcasted_iota(jnp.int32, (16, 768), 0) // 2) * 96
     mine = (lane >= first) & (lane < first + 96)
@@ -330,26 +348,23 @@
     return device(moved(c, "x", 2), core)
 
 
-def decode_mix(pk, qh, kh, vh, attn):
+def decode_mix(pk, qe, qo, kp, vp, attn):
     a = pk[4]
     acc, peak, total = a[:, :, 0:96], a[:, :, 96:97], a[:, :, 112:113]
-
-    def pairs(ref):
-        v = ref[:, 768:784, :].astype(F32)[:, 0:8, :]
-        return jnp.broadcast_to(v[:, None], (8, 2, 8, 96)).reshape(16, 8, 96)
-
-    q = qh[:, 768:784, :].astype(F32)[:, 0:8, :]
-    own = jnp.sum(q * pairs(kh), axis=-1, keepdims=True) * SCALE
+    q = decode_queries(qe, qo)
+    keys = jnp.stack([decode_rows(kp, h // 8, h % 8 // 2) for h in range(16)])
+    values = jnp.stack([vp[h // 8, 768:784, 96 * (h % 8 // 2) : 96 * (h % 8 // 2) + 96].astype(F32)[:8] for h in range(16)])
+    own = jnp.sum(q * keys, axis=-1, keepdims=True) * SCALE
     top = jnp.maximum(peak, own)
     old, new = jnp.exp(peak - top), jnp.exp(own - top)
-    mix = (acc * old + new * pairs(vh)) / (total * old + new)
+    mix = (acc * old + new * values) / (total * old + new)
     zero = jnp.zeros((8, 96), F32)
     for h in range(16):
         attn[768:784, 96 * h : 96 * h + 96] = jnp.concatenate([mix[h], zero], axis=0).astype(BF)
 
 
 def kernel(wq_ref, wo_ref, gain_ref, x_ref, dx_ref, freq, k_ref, v_ref, clen, out_ref, dout_ref,
-           own_q, own_o, other_q, other_o, gown, gother, w, g, xb, nb, u, cos, sin, qh, kh, vh, attn, kc, vc, o, pk, rv,
+           own_q, own_o, other_q, other_o, gown, gother, w, g, xb, nb, u, cos, sin, qe, qo, kp, vp, attn, kc, vc, o, pk, rv,
            ssem, rsem, ds, dr, ps, pr, gs, gr, cs, cr, lsem, osem):
     c, core = coords()
     loads = [pltpu.make_async_copy(s, d, lsem.at[i]) for i, (s, d) in enumerate((
@@ -376,50 +391,46 @@
     R = GainRing(g, gs, gr)
     D = Combine(pk, rv, cs, cr)
 
-    for tick in range(5):
+    def ticks(tick):
         R.step(tick)
         for t in range(N_CHUNK):
-            if tick == LAG * t:
+            if tick == t:
                 merge(t, own_q, other_q, own_o, other_o, w, c, core)
-            if 0 <= tick - LAG * t <= 6:
-                G.step(t, tick - LAG * t)
-    R.step(5)
+            if tick >= t:
+                G.step(t, tick - t)
+
+    for tick in range(5):
+        ticks(tick)
     angles(freq, clen, cos, sin)
-    R.step(6)
+    ticks(5)
     for cp in loads[2:4]:
         cp.wait()
+    R.step(6)
     normalize(xb, nb, gain_row(g))
-    G.step(0, 5)
-    G.step(1, 3)
-    G.step(2, 1)
     G.step(0, 6)
-    G.step(1, 4)
-    G.step(2, 2)
     G.take(0)
     project(nb, w, u, 0, 0, 3)
-    G.step(2, 3)
+    G.step(1, 5)
+    G.step(2, 4)
     project(nb, w, u, 0, 3, 6)
-    G.step(1, 5)
-    heads(u, cos, sin, qh, kh, vh, 0)
     G.step(1, 6)
-    G.step(2, 4)
-    attend(qh, kh, vh, attn, 0)
-    attend(qh, kh, vh, attn, 1)
+    heads(u, cos, sin, qe, qo, kp, vp, 0)
     G.step(2, 5)
-    attend(qh, kh, vh, attn, 2)
-    attend(qh, kh, vh, attn, 3)
+    attend(qe, qo, kp, vp, attn, 0)
+    G.take(1)
+    project(nb, w, u, 1, 0, 3)
     G.step(2, 6)
-    G.take(1)
-    project(nb, w, u, 1, 0, 6)
-    heads(u, cos, sin, qh, kh, vh, 1)
+    project(nb, w, u, 1, 3, 6)
+    heads(u, cos, sin, qe, qo, kp, vp, 1)
     for cp in loads[4:]:
         cp.wait()
-    decode_block(qh, kc, vc, clen, pk.at[0], None)
-    for j in range(4):
+    decode_block(qe, qo, kc, vc, clen, pk.at[0])
+    for j, groups in enumerate(((1, 2), (3, 4), (5, 6), (7,))):
         D.send(j)
-        attend(qh, kh, vh, attn, 4 + j)
+        for g_ in groups:
+            attend(qe, qo, kp, vp, attn, g_)
         D.add(j)
-    decode_mix(pk, qh, kh, vh, attn)
+    decode_mix(pk, qe, qo, kp, vp, attn)
     G.take(2)
 
     def leaving(j):
@@ -441,9 +452,6 @@
     D.finish()
     for cp in outs:
         cp.wait()
-
-
-LAG = 2
 
 
 def per_device(prefill_x, decode_x, norm_gain, wqkv, wo, k_cache, v_cache, cache_len):
@@ -463,7 +471,8 @@
             pltpu.VMEM((6 * n, 4, 2, 4, 2, 24, 256), BF), pltpu.VMEM((4, 2, 4, 2, 8, 128), BF),
             pltpu.VMEM((784, 1536), BF), pltpu.VMEM((784, 1536), BF), pltpu.VMEM((784, 1536), F32),
             pltpu.VMEM((784, 384), F32), pltpu.VMEM((784, 384), F32),
-            pltpu.VMEM((16, 784, 96), BF), pltpu.VMEM((8, 784, 96), BF), pltpu.VMEM((8, 784, 96), BF),
+            pltpu.VMEM((2, 784, 384), BF), pltpu.VMEM((2, 784, 384), BF),
+            pltpu.VMEM((2, 784, 384), BF), pltpu.VMEM((2, 784, 384), BF),
             pltpu.VMEM((784, 1536), BF), pltpu.VMEM((8, 512, 768), BF), pltpu.VMEM((8, 512, 768), BF),
             pltpu.VMEM((784, 1536), BF), pltpu.VMEM((5, 16, 8, 128), F32), pltpu.VMEM((4, 16, 8, 128), F32),
             dma((36 * n,)), dma((36 * n,)), dma((12 * n,)), dma((12 * n,)), dma((3,)), dma((3,)),

time: 101 us -> 89.4 us (0.89)
  Pallas kernels: 95.8 us -> 84.7 us
    pallas_call x1, Pallas kernels: 95.8 us -> 84.7 us  [per_device(): pl.pallas_call(kernel, out_shape=(jax.ShapeDtypeStruct((768, 1536), BF),...]
where the time goes in v3:
time: 89.4 us; the launch traced here: 89.2 us
  Pallas kernels  84.7 us (95%)
  local copies, waits for them, and re-layouts  3.84 us (4%)
    pallas_call x1, Pallas kernels, per_device(): pl.pallas_call(kernel, out_shape=(jax.ShapeDtypeStruct((768, 1536), BF),...  84.7 us
    unnamed x4, local copies, waits for them, and re-layouts  3.84 us

profile of v3, /device:TPU:0, one launch (start us, length us, event | category | flops | bytes accessed | tf_op | source)
XLA Modules:
  0.0 89.2 jit_solution(3172235116937120926)
XLA Ops:
  0.6 84.7 %sublayer.1 = (bf16[768,1536]{1,0:T(8,128)(2,1)}, bf16[8,1536]{1,0:T(8,128)(2,1)}) custom-call(bf16[12,3072]{1,0:T(8,128)(2,1)} %wq_ref.1, bf16[12,1536]{1,0:T(8,128)(2,1)} %wo_ref.1, bf16[1,12]{1,0:T(2,128)(2,1)} %bitcast.1, bf16[768,1536]{1,0:T(8,128)(2,1)} %x_ref.1, bf16[8,1536]{1,0:T(8,128)(2,1)} %dx_ref.1, f32[1,128]{1,0:T(1,128)} %constant.2.clone.freq, ...), custom_call_target="tpu_custom_call" | custom-call | tf_op jit(solution)/shard_map/sublayer/pallas_call | solution.py:463
  85.4 0.0 copy-start
  85.4 3.2 %copy.13 = bf16[768,1536]{1,0:T(8,128)(2,1)} copy(bf16[768,1536]{1,0:T(8,128)(2,1)} %get-tuple-element.4) | data formatting | bytes 4718592
  88.6 0.0 copy-done
  88.6 0.6 copy.14
Async XLA Ops:
  85.4 3.2 %copy-start = (bf16[8,1536]{1,0:T(8,128)(2,1)S(1)}, bf16[8,1536]{1,0:T(8,128)(2,1)}, u32[]{:S(2)}) copy-start(bf16[8,1536]{1,0:T(8,128)(2,1)} %get-tuple-element.5) | copy-start | bytes 73732

commit v4 on v3

--- a/solution.py
+++ b/solution.py
@@ -10,6 +10,7 @@
 H, KV, HD = 16, 8, 96
 THETA, EPS, NEGATIVE = 100000.0, 1e-05, -1e30
 SCALE = HD ** (-0.5)
+RATE = SCALE * 1.4426950408889634
 ORDERS = (("x", "y", "z"), ("y", "z", "x"), ("z", "x", "y"))
 N_CHUNK = 3
 BF, F32 = jnp.bfloat16, jnp.float32
@@ -223,9 +224,10 @@
     nb[768:784, :] = jnp.concatenate([scaled(768, 8), jnp.zeros((8, 1536), F32)], axis=0).astype(BF)
 
 
-def project(nb, w, u, t, lo, hi):
-    @pl.loop(lo, hi)
-    def _(j):
+def project(nb, w, u, t, core):
+    @pl.loop(0, 3)
+    def _(i):
+        j = core * 3 + i
         rhs = w[t * 6 + j].reshape(1536, 256)
         u[:, pl.ds(pl.multiple_of(j * 256, 256), 256)] = jnp.dot(nb[...], rhs, preferred_element_type=F32)
 
@@ -266,8 +268,7 @@
         column = lax.broadcasted_iota(jnp.int32, (512, 256), 1)
         last = jnp.where(column <= row, s[:, lo:n], NEGATIVE)
         s = jnp.concatenate([s[:, :lo], last], axis=1) if i else last
-        s = s * SCALE
-        e = jnp.exp(s - jnp.max(s, axis=-1, keepdims=True))
+        e = jnp.exp2(s * RATE - jnp.max(s, axis=-1, keepdims=True) * RATE)
         total = jnp.sum(e, axis=-1, keepdims=True)
         o = jnp.dot(e.astype(BF), vp[t, 0:n, win], preferred_element_type=F32)
         o = (o * (1.0 / total)).astype(BF)[:, off : off + 96]
@@ -380,8 +381,6 @@
         for i, (s, d) in enumerate(((wq_ref, other_q), (wo_ref, other_o), (gown, gother)))]
     for cp in pre:
         cp.start()
-    for cp in loads[2:]:
-        cp.start()
     for cp in loads[:2]:
         cp.wait()
     for cp in pre:
@@ -401,6 +400,9 @@
 
     for tick in range(5):
         ticks(tick)
+        if tick == 2:
+            for cp in loads[2:]:
+                cp.start()
     angles(freq, clen, cos, sin)
     ticks(5)
     for cp in loads[2:4]:
@@ -408,19 +410,19 @@
     R.step(6)
     normalize(xb, nb, gain_row(g))
     G.step(0, 6)
-    G.take(0)
-    project(nb, w, u, 0, 0, 3)
+    project(nb, w, u, 0, core)
     G.step(1, 5)
     G.step(2, 4)
-    project(nb, w, u, 0, 3, 6)
+    G.take(0)
+    project(nb, w, u, 0, 1 - core)
     G.step(1, 6)
     heads(u, cos, sin, qe, qo, kp, vp, 0)
     G.step(2, 5)
     attend(qe, qo, kp, vp, attn, 0)
+    project(nb, w, u, 1, core)
+    G.step(2, 6)
     G.take(1)
-    project(nb, w, u, 1, 0, 3)
-    G.step(2, 6)
-    project(nb, w, u, 1, 3, 6)
+    project(nb, w, u, 1, 1 - core)
     heads(u, cos, sin, qe, qo, kp, vp, 1)
     for cp in loads[4:]:
         cp.wait()

time: 89.4 us -> 89 us (level)
  no operation moved by 1% of the time
where the time goes in v4:
time: 89 us; the launch traced here: 88.9 us
  Pallas kernels  84.4 us (95%)
  local copies, waits for them, and re-layouts  3.84 us (4%)
    pallas_call x1, Pallas kernels, per_device(): pl.pallas_call(kernel, out_shape=(jax.ShapeDtypeStruct((768, 1536), BF),...  84.4 us
    unnamed x4, local copies, waits for them, and re-layouts  3.84 us

profile of v4, /device:TPU:0, one launch (start us, length us, event | category | flops | bytes accessed | tf_op | source)
XLA Modules:
  0.0 88.9 jit_solution(4121733255268158869)
XLA Ops:
  0.6 84.4 %sublayer.1 = (bf16[768,1536]{1,0:T(8,128)(2,1)}, bf16[8,1536]{1,0:T(8,128)(2,1)}) custom-call(bf16[12,3072]{1,0:T(8,128)(2,1)} %wq_ref.1, bf16[12,1536]{1,0:T(8,128)(2,1)} %wo_ref.1, bf16[1,12]{1,0:T(2,128)(2,1)} %bitcast.1, bf16[768,1536]{1,0:T(8,128)(2,1)} %x_ref.1, bf16[8,1536]{1,0:T(8,128)(2,1)} %dx_ref.1, f32[1,128]{1,0:T(1,128)} %constant.2.clone.freq, ...), custom_call_target="tpu_custom_call" | custom-call | tf_op jit(solution)/shard_map/sublayer/pallas_call | solution.py:465
  85.0 0.0 copy-start
  85.1 3.2 %copy.13 = bf16[768,1536]{1,0:T(8,128)(2,1)} copy(bf16[768,1536]{1,0:T(8,128)(2,1)} %get-tuple-element.4) | data formatting | bytes 4718592
  88.3 0.0 copy-done
  88.3 0.6 copy.14
Async XLA Ops:
  85.0 3.2 %copy-start = (bf16[8,1536]{1,0:T(8,128)(2,1)S(1)}, bf16[8,1536]{1,0:T(8,128)(2,1)}, u32[]{:S(2)}) copy-start(bf16[8,1536]{1,0:T(8,128)(2,1)} %get-tuple-element.5) | copy-start | bytes 73732

commit v5 on v4

--- a/solution.py
+++ b/solution.py
@@ -13,6 +13,7 @@
 RATE = SCALE * 1.4426950408889634
 ORDERS = (("x", "y", "z"), ("y", "z", "x"), ("z", "x", "y"))
 N_CHUNK = 3
+PLAN = ((0, 0), (1, 0), (1, 1), (2, 0), (2, 1))
 BF, F32 = jnp.bfloat16, jnp.float32
 
 
@@ -47,30 +48,28 @@
         core = self.core if core is None else core
         return self.w.at[t * 6 + core * 3 + k]
 
-    def copy(self, t, k, f, s, right, origin):
-        order = ORDERS[k]; axis = order[f]
+    def copy(self, t, k, f, s, by, origin):
+        order = ORDERS[k]
         b = block(self.part(t, k), origin, order[:f])
         if s == 1:
-            b = b.at[..., pl.ds(0 if right else 128, 128)]
-        i = (((t * 3 + k) * 3 + f) * 2 + s) * 2 + (0 if right else 1)
+            b = b.at[..., pl.ds(0 if by == 1 else 128, 128)]
+        i = (((t * 3 + k) * 3 + f) * 2 + (s if by != 2 else 1)) * 2 + (1 if by == -1 else 0)
         return pltpu.make_async_remote_copy(
             src_ref=b, dst_ref=b, send_sem=self.ssem.at[i], recv_sem=self.rsem.at[i],
-            device_id=device(moved(self.c, axis, 1 if right else -1), self.core), device_id_type=MESH)
+            device_id=device(moved(self.c, order[f], by), self.core), device_id_type=MESH)
 
     def send(self, t, f, s):
         for k in range(3):
-            axis = ORDERS[k][f]
-            for right in (True, False):
-                origin = self.c if s == 0 else moved(self.c, axis, -1 if right else 1)
-                cp = self.copy(t, k, f, s, right, origin)
-                cp.start(); self.sent.append(cp)
+            for by in (1, -1, 2) if f == 0 else (1, -1):
+                origin = self.c if s == 0 else moved(self.c, ORDERS[k][f], -by)
+                cp = self.copy(t, k, f, s, by, origin)
+                cp.start()
+                self.sent.append(cp)
 
     def recv(self, t, f, s):
         for k in range(3):
-            axis = ORDERS[k][f]
-            for right in (True, False):
-                by = (1 + s) * (-1 if right else 1)
-                self.copy(t, k, f, s, right, moved(self.c, axis, by)).wait_recv()
+            for by in (1, -1, 2) if f == 0 else (1, -1):
+                self.copy(t, k, f, s, by, moved(self.c, ORDERS[k][f], -(1 + s) * by)).wait_recv()
 
     def d2d(self, t, k, j, core):
         order = ORDERS[k]
@@ -92,14 +91,14 @@
 
     def step(self, t, n):
         if n > 0:
-            self.recv(t, (n - 1) // 2, (n - 1) % 2)
-        if n < 6:
-            self.send(t, n // 2, n % 2)
+            self.recv(t, *PLAN[n - 1])
+        if n < 5:
+            self.send(t, *PLAN[n])
+        if n == 3:
+            self.give(t, (0,))
         if n == 4:
-            self.give(t, (0,))
+            self.give(t, (1, 2))
         if n == 5:
-            self.give(t, (1, 2))
-        if n == 6:
             self.give(t, (3,))
 
     def finish(self):
@@ -111,13 +110,13 @@
     for axis in ("x", "y", "z"):
         for by in (1, -1):
             out.append(device(moved(c, axis, by), core))
-    return out + [partner(c, core, 1), partner(c, core, 3)]
+    return out + [device(moved(c, axis, 2), core) for axis in ("x", "y", "z")]
 
 def barrier(c, core):
     sem = pltpu.get_barrier_semaphore()
     for d in neighbours(c, core):
         pl.semaphore_signal(sem, inc=1, device_id=d, device_id_type=MESH)
-    pl.semaphore_wait(sem, 9)
+    pl.semaphore_wait(sem, 10)
 
 def both_rows(own, other, core):
     a, b = own[...].astype(F32), other[...].astype(F32)
@@ -171,24 +170,21 @@
         self.c, self.core = coords()
         self.sent = []
 
-    def copy(self, f, s, right, origin):
+    def copy(self, f, by, origin):
         order = ORDERS[0]
         b = block(self.g, origin, order[:f])
-        i = (f * 2 + s) * 2 + (0 if right else 1)
+        i = f * 4 + by + 1
         return pltpu.make_async_remote_copy(
             src_ref=b, dst_ref=b, send_sem=self.ssem.at[i], recv_sem=self.rsem.at[i],
-            device_id=device(moved(self.c, order[f], 1 if right else -1), self.core), device_id_type=MESH)
+            device_id=device(moved(self.c, order[f], by), self.core), device_id_type=MESH)
 
     def step(self, n):
-        axes = ORDERS[0]
         if n > 0:
-            f, s = (n - 1) // 2, (n - 1) % 2
-            for right in (True, False) if s == 0 else (True,):
-                self.copy(f, s, right, moved(self.c, axes[f], (1 + s) * (-1 if right else 1))).wait_recv()
-        if n < 6:
-            f, s = n // 2, n % 2
-            for right in (True, False) if s == 0 else (True,):
-                cp = self.copy(f, s, right, self.c if s == 0 else moved(self.c, axes[f], -1))
+            for by in (1, -1, 2):
+                self.copy(n - 1, by, moved(self.c, ORDERS[0][n - 1], -by)).wait_recv()
+        if n < 3:
+            for by in (1, -1, 2):
+                cp = self.copy(n, by, self.c)
                 cp.start()
                 self.sent.append(cp)
 
@@ -391,36 +387,36 @@
     D = Combine(pk, rv, cs, cr)
 
     def ticks(tick):
-        R.step(tick)
+        if tick < 4:
+            R.step(tick)
         for t in range(N_CHUNK):
             if tick == t:
                 merge(t, own_q, other_q, own_o, other_o, w, c, core)
             if tick >= t:
                 G.step(t, tick - t)
 
-    for tick in range(5):
+    for tick in range(4):
         ticks(tick)
         if tick == 2:
             for cp in loads[2:]:
                 cp.start()
     angles(freq, clen, cos, sin)
-    ticks(5)
+    ticks(4)
     for cp in loads[2:4]:
         cp.wait()
-    R.step(6)
     normalize(xb, nb, gain_row(g))
-    G.step(0, 6)
+    G.step(0, 5)
     project(nb, w, u, 0, core)
-    G.step(1, 5)
-    G.step(2, 4)
+    G.step(1, 4)
+    G.step(2, 3)
     G.take(0)
     project(nb, w, u, 0, 1 - core)
-    G.step(1, 6)
+    G.step(1, 5)
     heads(u, cos, sin, qe, qo, kp, vp, 0)
-    G.step(2, 5)
+    G.step(2, 4)
     attend(qe, qo, kp, vp, attn, 0)
     project(nb, w, u, 1, core)
-    G.step(2, 6)
+    G.step(2, 5)
     G.take(1)
     project(nb, w, u, 1, 1 - core)
     heads(u, cos, sin, qe, qo, kp, vp, 1)

time: 89 us -> 85.4 us (0.960)
  Pallas kernels: 84.4 us -> 80.8 us
    pallas_call x1, Pallas kernels: 84.4 us -> 80.8 us  [per_device(): pl.pallas_call(kernel, out_shape=(jax.ShapeDtypeStruct((768, 1536), BF),...]
where the time goes in v5:
time: 85.4 us; the launch traced here: 85.2 us
  Pallas kernels  80.8 us (95%)
  local copies, waits for them, and re-layouts  3.84 us (4%)
    pallas_call x1, Pallas kernels, per_device(): pl.pallas_call(kernel, out_shape=(jax.ShapeDtypeStruct((768, 1536), BF),...  80.8 us
    unnamed x4, local copies, waits for them, and re-layouts  3.84 us

profile of v5, /device:TPU:0, one launch (start us, length us, event | category | flops | bytes accessed | tf_op | source)
XLA Modules:
  0.0 85.2 jit_solution(5919121070395087634)
XLA Ops:
  0.6 80.8 %sublayer.1 = (bf16[768,1536]{1,0:T(8,128)(2,1)}, bf16[8,1536]{1,0:T(8,128)(2,1)}) custom-call(bf16[12,3072]{1,0:T(8,128)(2,1)} %wq_ref.1, bf16[12,1536]{1,0:T(8,128)(2,1)} %wo_ref.1, bf16[1,12]{1,0:T(2,128)(2,1)} %bitcast.1, bf16[768,1536]{1,0:T(8,128)(2,1)} %x_ref.1, bf16[8,1536]{1,0:T(8,128)(2,1)} %dx_ref.1, f32[1,128]{1,0:T(1,128)} %constant.2.clone.freq, ...), custom_call_target="tpu_custom_call" | custom-call | tf_op jit(solution)/shard_map/sublayer/pallas_call | solution.py:461
  81.4 0.0 copy-start
  81.4 3.2 %copy.13 = bf16[768,1536]{1,0:T(8,128)(2,1)} copy(bf16[768,1536]{1,0:T(8,128)(2,1)} %get-tuple-element.4) | data formatting | bytes 4718592
  84.6 0.0 copy-done
  84.6 0.6 copy.14
Async XLA Ops:
  81.4 3.2 %copy-start = (bf16[8,1536]{1,0:T(8,128)(2,1)S(1)}, bf16[8,1536]{1,0:T(8,128)(2,1)}, u32[]{:S(2)}) copy-start(bf16[8,1536]{1,0:T(8,128)(2,1)} %get-tuple-element.5) | copy-start | bytes 73732
